TPU v7x, 32 devices: a whole 2x2x4 slice. The times are simulated.
32 devices in a mesh: range: 4 (over z), doppler: 8 (over y, x, core).
Axes of the slice: x: 2, y: 2, z: 4, core: 2. Of those that a mesh axis runs over, the one named last changes fastest.
Arguments:
- snapshot: bfloat16 [2, 2048, 2, 64, 128], P(None, ('range', 'doppler')), may hold values from -120 to 120
- spatial: bfloat16 [2, 128, 2, 128], replicated, may hold values from -0.375 to 0.375
- tap_weights: float32 [64, 2, 3, 128], P('doppler'), may hold values from -6 to 6
- step_size: float32 [64], P('doppler'), may hold values from 0.2 to 0.8
- train_mask: int32 [2, 2048], P(None, 'range'), may hold values 0 or 1
- guard_center: int32 [2], replicated, may hold values from 0 to 2047
Outputs:
- errors: float32 [2, 2, 64, 2048], P(None, None, 'doppler', 'range')
- final_taps: float32 [64, 2, 3, 128], P('doppler')
All inputs are finite; a program needn't handle non-finite values. No bound on the sum of `train_mask` on one device may be relied on, other than what follows from the above.
Results may differ from a plain program's by a relative error of at most 0.0057.
Values may be sent and summed in bfloat16 or wider, within the bound.
A program may use at most 64 MiB of HBM per device.

v0:
```python
import math

import jax
import jax.numpy as jnp
from jax import lax
from jax.sharding import PartitionSpec as P


def padded(array, sides, width):
    for axis, dim in sides:
        size, length = (lax.axis_size(axis), array.shape[dim])
        up = [(i, (i + 1) % size) for i in range(size)]
        down = [(j, i) for i, j in up]
        last = lax.slice_in_dim(array, length - width, length, axis=dim)
        leading = lax.slice_in_dim(array, 0, width, axis=dim)
        before = lax.ppermute(last, axis, up)
        after = lax.ppermute(leading, axis, down)
        array = jnp.concatenate([before, array, after], axis=dim)
    return array


def dft_table(pulse_count):
    sample_index = jnp.arange(pulse_count, dtype=jnp.int32)
    phase_index = sample_index[:, None] * sample_index[None, :] % pulse_count
    angles = phase_index.astype(jnp.float32) * (2.0 * math.pi / pulse_count)
    cosine = jnp.cos(angles) / math.sqrt(pulse_count)
    sine_part = jnp.sin(angles) / math.sqrt(pulse_count)
    upper_rows = jnp.stack([cosine, -sine_part], axis=1)
    lower_rows = jnp.stack([sine_part, cosine], axis=1)
    return jnp.stack([upper_rows, lower_rows], axis=0).astype(jnp.bfloat16)


def to_bins(samples, spatial, transform):
    beam_data = jnp.einsum(
        "grpc,rcsb->gspb", samples, spatial, preferred_element_type=jnp.float32
    ).astype(jnp.bfloat16)
    return jnp.einsum(
        "gspb,sptk->gtkb", beam_data, transform, preferred_element_type=jnp.float32
    ).astype(jnp.bfloat16)


def tap_terms(extended):
    bin_width = extended.shape[2] - 2
    auxiliary = jnp.stack(
        [extended[:, :, offset : offset + bin_width] for offset in range(3)], axis=3
    )
    beam_index = jnp.arange(auxiliary.shape[4], dtype=jnp.int32)
    tap_index = jnp.arange(3, dtype=jnp.int32)
    live_slots = jnp.logical_or(tap_index[:, None] != 1, beam_index[None, :] != 0)
    auxiliary = jnp.where(live_slots, auxiliary, jnp.zeros_like(auxiliary))
    main_beam = extended[:, :, 1 : 1 + bin_width, 0]
    return (auxiliary, main_beam)


def canceller(extended, weights, trained):
    auxiliary, main_beam = tap_terms(extended)
    scaling = 1.0 / math.sqrt(3 * auxiliary.shape[4])
    filtered = jnp.einsum(
        "rskjb,kqjb->rskq", auxiliary, weights, preferred_element_type=jnp.float32
    )
    real_part = filtered[:, 0, :, 0] + filtered[:, 1, :, 1]
    imag_part = filtered[:, 1, :, 0] - filtered[:, 0, :, 1]
    main_wide = main_beam.astype(jnp.float32)
    errors = jnp.stack(
        [main_wide[:, 0] - scaling * real_part, main_wide[:, 1] - scaling * imag_part], axis=1
    )
    weighted = errors.astype(jnp.bfloat16) * trained.astype(jnp.bfloat16)[:, None, None]
    cross_sum = jnp.einsum(
        "rqk,rskjb->kqsjb", weighted, auxiliary, preferred_element_type=jnp.float32
    )
    gradient = jnp.stack(
        [cross_sum[:, 0, 0] + cross_sum[:, 1, 1], cross_sum[:, 0, 1] - cross_sum[:, 1, 0]], axis=1
    )
    energy = jnp.einsum("rskjb,rskjb->rk", auxiliary, auxiliary, preferred_element_type=jnp.float32)
    power_sum = jnp.einsum("r,rk->k", trained.astype(jnp.float32), energy)
    return (jnp.transpose(errors, (1, 2, 0)), gradient, power_sum)


def advance(current, steps, gradient, power_sum):
    slot_count = 3 * current.shape[3]
    normalizer = power_sum / slot_count + 1e-06
    factor = steps * math.sqrt(slot_count) / normalizer
    return current + factor[:, None, None, None] * gradient


def training(mask_row, positions, centre_gate, guard_width):
    outside = jnp.abs(positions - centre_gate) > guard_width
    return jnp.where(outside, mask_row, 0)


def body(snapshot, spatial, tap_weights, step_size, train_mask, guard_center):
    transform = dft_table(snapshot.shape[3])
    range_count = lax.axis_size("range")
    doppler_count = lax.axis_size("doppler")
    gate_count = snapshot.shape[1]
    guard_width = gate_count * range_count * doppler_count // 8
    outputs = []
    range_gates = gate_count * doppler_count
    positions = lax.axis_index("range") * range_gates + jnp.arange(range_gates, dtype=jnp.int32)
    current = tap_weights
    for block_index in range(snapshot.shape[0]):
        spectra = to_bins(snapshot[block_index], spatial, transform)
        owned_bins = lax.all_to_all(spectra, "doppler", split_axis=2, concat_axis=0, tiled=True)
        extended = padded(owned_bins, (("doppler", 2),), 1)
        trained = training(
            train_mask[block_index], positions, guard_center[block_index], guard_width
        )
        errors, gradient, power_sum = canceller(extended, current.astype(jnp.bfloat16), trained)
        gradient, power_sum = lax.psum((gradient, power_sum), "range")
        current = advance(current, step_size, gradient, power_sum)
        outputs.append(errors)
    return (jnp.stack(outputs), current)


def solution(mesh):
    return jax.shard_map(
        body,
        mesh=mesh,
        in_specs=(
            P(None, ("range", "doppler"), None, None, None),
            P(),
            P("doppler", None, None, None),
            P("doppler"),
            P(None, "range"),
            P(),
        ),
        out_specs=(P(None, None, "doppler", "range"), P("doppler", None, None, None)),
        check_vma=False,
    )
```

profile of v0, /device:TPU:0, one launch (start us, length us, event | category | flops | bytes accessed | tf_op | source)
XLA Modules:
  0.0 154.2 jit_solution(18322434615055696131)
XLA Ops:
  1.0 3.1 %fusion.23 = bf16[64,2,64,128]{3,2,0,1:T(8,128)(2,1)S(1)} fusion(bf16[2,64,2,64,128]{4,3,2,1,0:T(8,128)(2,1)} %param.6, bf16[2,128,2,128]{3,2,1,0:T(2,128)(2,1)} %param.7, bf16[1,64,2,64]{1,3,0,2:T(8,128)(2,1)S(1)} %get-tuple-element.35, bf16[1,64,2,64]{1,3,0,2:T(8,128)(2,1)S(1)} %get-tuple-element.34), kind=kOutput, calls=%fused_computation.33 | convolution fusion | flops 807469056 | bytes 4358144 | tf_op jit(solution)/shard_map/gspb,sptk->gtkb/dot_general | solution.py:37
  4.0 2.7 %copy.63 = bf16[64,2,64,128]{3,0,1,2:T(8,128)(2,1)} copy(bf16[64,2,64,128]{3,2,0,1:T(8,128)(2,1)S(1)} %fusion.23) | data formatting | bytes 4194304 | tf_op jit(solution)/shard_map/convert_element_type | solution.py:39
  6.7 5.2 %all-to-all-start.1 = ((bf16[64,2,64,128]{3,0,1,2:T(8,128)(2,1)}), bf16[64,2,64,128]{3,0,1,2:T(8,128)(2,1)S(1)}, u32[]{:S(2)}, u32[]{:S(2)}) async-start(bf16[64,2,64,128]{3,0,1,2:T(8,128)(2,1)} %copy.63), calls=%async_computation.1 | async-start | bytes 4194304 | tf_op jit(solution)/shard_map/all_to_all | solution.py:103
  11.9 4.3 %fusion.20 = bf16[64,2,64,128]{3,2,0,1:T(8,128)(2,1)} fusion(bf16[2,64,2,64,128]{4,3,2,1,0:T(8,128)(2,1)} %param.6, bf16[2,128,2,128]{3,2,1,0:T(2,128)(2,1)S(1)} %copy-done.6, bf16[1,64,2,64]{1,3,0,2:T(8,128)(2,1)S(1)} %get-tuple-element.35, bf16[1,64,2,64]{1,3,0,2:T(8,128)(2,1)S(1)} %get-tuple-element.34), kind=kOutput, calls=%fused_computation.32 | convolution fusion | flops 807469056 | bytes 4358144 | tf_op jit(solution)/shard_map/gspb,sptk->gtkb/dot_general | solution.py:37
  16.3 4.3 %copy.53 = bf16[64,2,64,128]{3,0,1,2:T(8,128)(2,1)} copy(bf16[64,2,64,128]{3,2,0,1:T(8,128)(2,1)} %fusion.20) | data formatting | bytes 4194304 | tf_op jit(solution)/shard_map/convert_element_type | solution.py:39
  20.6 17.9 %all-to-all-done.1 = bf16[64,2,64,128]{3,0,1,2:T(8,128)(2,1)S(1)} async-done(((bf16[64,2,64,128]{3,0,1,2:T(8,128)(2,1)}), bf16[64,2,64,128]{3,0,1,2:T(8,128)(2,1)S(1)}, u32[]{:S(2)}, u32[]{:S(2)}) %all-to-all-start.1) | async-done | bytes 2097184 | tf_op jit(solution)/shard_map/all_to_all | solution.py:103
  38.5 4.3 %all-to-all-start = ((bf16[64,2,64,128]{3,0,1,2:T(8,128)(2,1)}), bf16[64,2,64,128]{3,0,1,2:T(8,128)(2,1)}, u32[]{:S(2)}, u32[]{:S(2)}) async-start(bf16[64,2,64,128]{3,0,1,2:T(8,128)(2,1)} %copy.53), calls=%async_computation | async-start | bytes 4194304 | tf_op jit(solution)/shard_map/all_to_all | solution.py:103
  42.9 0.6 fusion.91
  43.6 1.3 fusion.81
  44.9 3.0 %copy.65 = bf16[8,64,2,8,128]{4,3,2,1,0:T(8,128)(2,1)S(1)} copy(bf16[8,64,2,8,128]{4,1,2,3,0:T(8,128)(2,1)} %bitcast.210) | data formatting | bytes 4194304 | tf_op jit(solution)/shard_map/all_to_all | solution.py:103
  47.9 1.7 %fusion.89 = (bf16[512,2,1,128]{3,2,1,0:T(2,128)(2,1)}, bf16[512,2,1,128]{3,2,1,0:T(2,128)(2,1)}) fusion(bf16[512,2,8,128]{3,2,1,0:T(8,128)(2,1)S(1)} %bitcast.202), kind=kLoop, calls=%fused_computation.123 | loop fusion | bytes 1048576 | tf_op jit(solution)/shard_map/slice | solution.py:14
  49.5 0.4 collective-permute-start.2
  49.9 2.3 %collective-permute-start.3 = (bf16[512,2,1,128]{3,2,1,0:T(2,128)(2,1)}, bf16[512,2,1,128]{3,2,1,0:T(2,128)(2,1)S(1)}, u32[]{:S(2)}, u32[]{:S(2)}) collective-permute-start(bf16[512,2,1,128]{3,2,1,0:T(2,128)(2,1)} %get-tuple-element.25), channel_id=1, source_target_pairs={{1,0},{2,1},{3,2},{4,3},{5,4},{6,5},{7,6},{0,7},{9,8},{10,9},{11,1... | collective-permute-start | bytes 786440 | tf_op jit(solution)/shard_map/ppermute | solution.py:17
  52.2 17.9 %all-to-all-done = bf16[64,2,64,128]{3,0,1,2:T(8,128)(2,1)} async-done(((bf16[64,2,64,128]{3,0,1,2:T(8,128)(2,1)}), bf16[64,2,64,128]{3,0,1,2:T(8,128)(2,1)}, u32[]{:S(2)}, u32[]{:S(2)}) %all-to-all-start) | async-done | bytes 2097184 | tf_op jit(solution)/shard_map/all_to_all | solution.py:103
  70.1 3.0 %copy.55 = bf16[8,64,2,8,128]{4,3,2,1,0:T(8,128)(2,1)S(1)} copy(bf16[8,64,2,8,128]{4,1,2,3,0:T(8,128)(2,1)} %bitcast.22) | data formatting | bytes 4194304 | tf_op jit(solution)/shard_map/all_to_all | solution.py:103
  73.0 1.3 copy-done
  74.4 1.7 %fusion.88 = (bf16[512,2,1,128]{3,2,1,0:T(2,128)(2,1)}, bf16[512,2,1,128]{3,2,1,0:T(2,128)(2,1)}) fusion(bf16[512,2,8,128]{3,2,1,0:T(8,128)(2,1)S(1)} %bitcast.206), kind=kLoop, calls=%fused_computation.122 | loop fusion | bytes 1048576 | tf_op jit(solution)/shard_map/slice | solution.py:14
  76.0 2.6 %collective-permute-start.1 = (bf16[512,2,1,128]{3,2,1,0:T(2,128)(2,1)}, bf16[512,2,1,128]{3,2,1,0:T(2,128)(2,1)}, u32[]{:S(2)}, u32[]{:S(2)}) collective-permute-start(bf16[512,2,1,128]{3,2,1,0:T(2,128)(2,1)} %get-tuple-element.21), channel_id=1, source_target_pairs={{1,0},{2,1},{3,2},{4,3},{5,4},{6,5},{7,6},{0,7},{9,8},{10,9},{11,1... | collective-permute-start | bytes 786440 | tf_op jit(solution)/shard_map/ppermute | solution.py:17
  78.7 3.2 %copy.102 = bf16[512,2,8,1]{0,1,2,3:T(2,128)(2,1)S(1)} copy(bf16[512,2,8,1]{3,2,1,0:T(8,128)(2,1)} %bitcast.207) | data formatting | bytes 32768
  81.9 1.8 %copy.105 = bf16[512,2,8,1]{0,1,2,3:T(2,128)(2,1)S(1)} copy(bf16[512,2,8,1]{3,2,1,0:T(8,128)(2,1)S(1)} %bitcast.203) | data formatting | bytes 32768
  83.7 2.1 %fusion.11 = (bf16[512,2,8,1,128]{4,2,1,0,3:T(8,128)(2,1)S(1)}, bf16[512,2,8,1,128]{4,2,1,0,3:T(8,128)(2,1)S(1)}) fusion(bf16[512,2,8,128]{3,2,1,0:T(8,128)(2,1)S(1)} %bitcast.204, bf16[512,2,1,128]{3,2,1,0:T(2,128)(2,1)S(1)} %collective-permute-done.2, bf16[512,2,1,128]{3,2,1,0:T(2,128)(2,1)S(1)} %collective-permute-done.3), kind=kLoop, calls=%fused_computation.21 | loop fusion | flops 8388608 | bytes 6815744 | tf_op jit(solution)/shard_map/stack | solution.py:44
  85.8 5.6 %collective-permute-done = bf16[512,2,1,128]{3,2,1,0:T(2,128)(2,1)} collective-permute-done((bf16[512,2,1,128]{3,2,1,0:T(2,128)(2,1)}, bf16[512,2,1,128]{3,2,1,0:T(2,128)(2,1)}, u32[]{:S(2)}, u32[]{:S(2)}) %collective-permute-start) | collective-permute-done | bytes 262176 | tf_op jit(solution)/shard_map/ppermute | solution.py:16
  91.5 3.1 %fusion.13 = (bf16[512,2,8,1,128]{4,2,1,0,3:T(8,128)(2,1)S(1)}, bf16[512,2,8,1,128]{4,2,1,0,3:T(8,128)(2,1)S(1)}) fusion(bf16[512,2,8,128]{3,2,1,0:T(8,128)(2,1)S(1)} %bitcast.208, bf16[512,2,1,128]{3,2,1,0:T(2,128)(2,1)} %collective-permute-done, bf16[512,2,1,128]{3,2,1,0:T(2,128)(2,1)} %collective-permute-done.1), kind=kLoop, calls=%fused_computation.25 | loop fusion | flops 8388608 | bytes 6815744 | tf_op jit(solution)/shard_map/stack | solution.py:44
  94.6 6.0 %fusion.1 = (bf16[512,8]{1,0:T(8,128)(2,1)S(1)}, bf16[512,2,8,3,128]{4,2,1,0,3:T(8,128)(2,1)S(1)}, bf16[512,8]{1,0:T(8,128)(2,1)S(1)}, bf16[512,2,8,3,128]{4,2,1,0,3:T(8,128)(2,1)}) fusion(bf16[512,2,8,1,128]{4,2,1,0,3:T(8,128)(2,1)S(1)} %get-tuple-element.19, bf16[512,2,8,1,128]{4,2,1,0,3:T(8,128)(2,1)S(1)} %bitcast.209, ...), kind=kLoop, calls=%fused_computation.3 | loop fusion | flops 62906368 | bytes 25182592 | tf_op jit(solution)/shard_map/rskjb,rskjb->rk/dot_general | solution.py:74
  100.6 3.2 %fusion.34 = f32[512,2,8,2]{0,3,1,2:T(2,128)S(1)} fusion(bf16[512,2,8,3,128]{4,2,1,0,3:T(8,128)(2,1)S(1)} %get-tuple-element.17, f32[8,2,3,128]{3,1,2,0:T(2,128)S(1)} %copy-done.3), kind=kOutput, calls=%fused_computation.34 | convolution fusion | flops 12589056 | bytes 6381568 | tf_op jit(solution)/shard_map/rskjb,kqjb->rskq/dot_general | solution.py:58
  103.9 2.3 %fusion.6 = f32[8,2,2,3,128]{4,1,3,2,0:T(2,128)S(1)} fusion(bf16[512,2,8,3,128]{4,2,1,0,3:T(8,128)(2,1)S(1)} %get-tuple-element.17, f32[512,1,8]{0,1,2:T(1,128)S(1)} %get-tuple-element.29, f32[512,1,8]{0,1,2:T(1,128)S(1)} %get-tuple-element.28, bf16[512]{0:T(512)(128)(2,1)S(1)} %get-tuple-element.48), kind=kOutput, calls=%fused_computation.10 | convolution fusion | flops 12632064 | bytes 6374400 | tf_op jit(solution)/shard_map/rqk,rskjb->kqsjb/dot_general | solution.py:68
  106.3 19.3 %all-reduce.1 = (f32[8,2,3,128]{3,1,2,0:T(2,128)S(1)}, f32[8]{0:T(128)S(1)}) all-reduce(f32[8,2,3,128]{3,1,2,0:T(2,128)S(1)} %pad_maximum_fusion.7, f32[8]{0:T(128)S(1)} %convolution_bitcast_fusion.1), channel_id=1, replica_groups=mesh['range'=4,'doppler'=8] {'range'}, use_global_device_ids=true, to_apply=%region_1.2 | all-reduce | flops 6152 | bytes 49216 | tf_op jit(solution)/shard_map/psum | solution.py:109
  125.7 6.0 %fusion.37 = f32[8,2,512,2]{2,1,3,0:T(2,128)S(1)} fusion(bf16[512,2,8,3,128]{4,2,1,0,3:T(8,128)(2,1)} %get-tuple-element.45, f32[8,2,3,128]{3,1,2,0:T(2,128)S(1)} %multiply_add_fusion.1), kind=kOutput, calls=%fused_computation.35 | convolution fusion | flops 12589056 | bytes 6381568 | tf_op jit(solution)/shard_map/rskjb,kqjb->rskq/dot_general | solution.py:58
  131.8 5.0 %fusion.2 = f32[8,2,2,3,128]{4,1,3,2,0:T(2,128)S(1)} fusion(bf16[512,2,8,3,128]{4,2,1,0,3:T(8,128)(2,1)} %get-tuple-element.45, f32[512,1,8]{0,1,2:T(1,128)S(1)} %get-tuple-element.27, f32[512,1,8]{0,1,2:T(1,128)S(1)} %get-tuple-element.26, bf16[512]{0:T(512)(128)(2,1)S(1)} %get-tuple-element.39), kind=kOutput, calls=%fused_computation.6 | convolution fusion | flops 12632064 | bytes 6374400 | tf_op jit(solution)/shard_map/rqk,rskjb->kqsjb/dot_general | solution.py:68
  137.1 15.8 %all-reduce = (f32[8,2,3,128]{3,1,2,0:T(2,128)S(1)}, f32[8]{0:T(128)S(1)}) all-reduce(f32[8,2,3,128]{3,1,2,0:T(2,128)S(1)} %pad_maximum_fusion.8, f32[8]{0:T(128)S(1)} %convolution_bitcast_fusion), channel_id=1, replica_groups=mesh['range'=4,'doppler'=8] {'range'}, use_global_device_ids=true, to_apply=%region_3.4 | all-reduce | flops 6152 | bytes 49216 | tf_op jit(solution)/shard_map/psum | solution.py:109
  152.9 0.6 copy.72
  153.5 0.7 multiply_add_fusion
  (43 shorter events, 1.2 us)
Async XLA Ops:
  4.0 7.9 %copy-start.6 = (bf16[2,128,2,128]{3,2,1,0:T(2,128)(2,1)S(1)}, bf16[2,128,2,128]{3,2,1,0:T(2,128)(2,1)}, u32[]{:S(2)}) copy-start(bf16[2,128,2,128]{3,2,1,0:T(2,128)(2,1)} %param.7) | copy-start | bytes 393220
  6.7 31.8 %all-to-all-start.1 = ((bf16[64,2,64,128]{3,0,1,2:T(8,128)(2,1)}), bf16[64,2,64,128]{3,0,1,2:T(8,128)(2,1)S(1)}, u32[]{:S(2)}, u32[]{:S(2)}) async-start(bf16[64,2,64,128]{3,0,1,2:T(8,128)(2,1)} %copy.63), calls=%async_computation.1 | async-start | bytes 4194304 | tf_op jit(solution)/shard_map/all_to_all | solution.py:103
  16.3 26.6 %copy-start.5 = (s32[2]{0:T(128)S(1)}, s32[2]{0:T(128)}, u32[]{:S(2)}) copy-start(s32[2]{0:T(128)} %param.11) | copy-start | bytes 28
  16.3 27.3 %copy-start.4 = (s32[2,512]{1,0:T(2,128)S(1)}, s32[2,512]{1,0:T(2,128)}, u32[]{:S(2)}) copy-start(s32[2,512]{1,0:T(2,128)} %param.10) | copy-start | bytes 12292
  38.5 6.4 %copy-start.2 = (bf16[64,2,64,128]{3,0,1,2:T(8,128)(2,1)}, bf16[64,2,64,128]{3,0,1,2:T(8,128)(2,1)S(1)}, u32[]{:S(2)}) copy-start(bf16[64,2,64,128]{3,0,1,2:T(8,128)(2,1)S(1)} %all-to-all-done.1) | copy-start | bytes 6291460
  38.5 31.5 %all-to-all-start = ((bf16[64,2,64,128]{3,0,1,2:T(8,128)(2,1)}), bf16[64,2,64,128]{3,0,1,2:T(8,128)(2,1)}, u32[]{:S(2)}, u32[]{:S(2)}) async-start(bf16[64,2,64,128]{3,0,1,2:T(8,128)(2,1)} %copy.53), calls=%async_computation | async-start | bytes 4194304 | tf_op jit(solution)/shard_map/all_to_all | solution.py:103
  49.5 34.2 %collective-permute-start.2 = (bf16[512,2,1,128]{3,2,1,0:T(2,128)(2,1)}, bf16[512,2,1,128]{3,2,1,0:T(2,128)(2,1)S(1)}, u32[]{:S(2)}, u32[]{:S(2)}) collective-permute-start(bf16[512,2,1,128]{3,2,1,0:T(2,128)(2,1)} %get-tuple-element.24), channel_id=1, source_target_pairs={{0,1},{1,2},{2,3},{3,4},{4,5},{5,6},{6,7},{7,0},{8,9},{9,10},{10,1... | collective-permute-start | bytes 786440 | tf_op jit(solution)/shard_map/ppermute | solution.py:16
  49.9 33.8 %collective-permute-start.3 = (bf16[512,2,1,128]{3,2,1,0:T(2,128)(2,1)}, bf16[512,2,1,128]{3,2,1,0:T(2,128)(2,1)S(1)}, u32[]{:S(2)}, u32[]{:S(2)}) collective-permute-start(bf16[512,2,1,128]{3,2,1,0:T(2,128)(2,1)} %get-tuple-element.25), channel_id=1, source_target_pairs={{1,0},{2,1},{3,2},{4,3},{5,4},{6,5},{7,6},{0,7},{9,8},{10,9},{11,1... | collective-permute-start | bytes 786440 | tf_op jit(solution)/shard_map/ppermute | solution.py:17
  73.0 1.3 copy-start
  76.0 15.4 %collective-permute-start = (bf16[512,2,1,128]{3,2,1,0:T(2,128)(2,1)}, bf16[512,2,1,128]{3,2,1,0:T(2,128)(2,1)}, u32[]{:S(2)}, u32[]{:S(2)}) collective-permute-start(bf16[512,2,1,128]{3,2,1,0:T(2,128)(2,1)} %get-tuple-element.20), channel_id=1, source_target_pairs={{0,1},{1,2},{2,3},{3,4},{4,5},{5,6},{6,7},{7,0},{8,9},{9,10},{10,1... | collective-permute-start | bytes 786440 | tf_op jit(solution)/shard_map/ppermute | solution.py:16
  76.0 15.4 %collective-permute-start.1 = (bf16[512,2,1,128]{3,2,1,0:T(2,128)(2,1)}, bf16[512,2,1,128]{3,2,1,0:T(2,128)(2,1)}, u32[]{:S(2)}, u32[]{:S(2)}) collective-permute-start(bf16[512,2,1,128]{3,2,1,0:T(2,128)(2,1)} %get-tuple-element.21), channel_id=1, source_target_pairs={{1,0},{2,1},{3,2},{4,3},{5,4},{6,5},{7,6},{0,7},{9,8},{10,9},{11,1... | collective-permute-start | bytes 786440 | tf_op jit(solution)/shard_map/ppermute | solution.py:17
  83.7 7.8 %copy-start.1 = (bf16[8,64,2,8,128]{4,3,2,1,0:T(8,128)(2,1)S(1)}, bf16[8,64,2,8,128]{4,3,2,1,0:T(8,128)(2,1)}, u32[]{:S(2)}) copy-start(bf16[8,64,2,8,128]{4,3,2,1,0:T(8,128)(2,1)} %copy-done) | copy-start | bytes 6291460
  94.6 6.0 %copy-start.3 = (f32[8,2,3,128]{3,1,2,0:T(2,128)S(1)}, f32[8,2,3,128]{3,1,2,0:T(2,128)}, u32[]{:S(2)}) copy-start(f32[8,2,3,128]{3,1,2,0:T(2,128)} %param.8) | copy-start | bytes 73732
  103.8 21.9 %copy-start.7 = (f32[8]{0:T(128)S(1)}, f32[8]{0:T(128)}, u32[]{:S(2)}) copy-start(f32[8]{0:T(128)} %param.9) | copy-start | bytes 100
where the time goes:
time: 155 us; the launch traced here: 154 us
  waiting for transfers between devices  41.5 us (27%)
  blocking collectives  35.1 us (23%)
  matrix products  24.1 us (16%)
  local copies, waits for them, and re-layouts  23.8 us (15%)
  starting transfers between devices  14.8 us (10%)
  other arithmetic  14 us (9%)
    all_to_all x2, waiting for transfers between devices, body(): lax.all_to_all(spectra, 'doppler', split_axis=2, concat_axis=0, tiled=True)  35.8 us
    psum x2, blocking collectives, body(): gradient, power_sum = lax.psum((gradient, power_sum), 'range')  35.1 us
    all_to_all x2, starting transfers between devices, body(): lax.all_to_all(spectra, 'doppler', split_axis=2, concat_axis=0, tiled=True)  9.54 us
    dot_general x2, matrix products, canceller(): jnp.einsum('rskjb,kqjb->rskq', auxiliary, weights, preferred_element_type...  9.12 us
    dot_general x2, matrix products, to_bins(): jnp.einsum('gspb,sptk->gtkb', beam_data, transform, preferred_element_typ...  7.42 us
    dot_general x2, matrix products, canceller(): jnp.einsum('rqk,rskjb->kqsjb', weighted, auxiliary, preferred_element_typ...  7.3 us
    unnamed x19, local copies, waits for them, and re-layouts  6.99 us
    convert_element_type x2, local copies, waits for them, and re-layouts, to_bins(): return jnp.einsum('gspb,sptk->gtkb', beam_data, transform, preferred_elem...  6.97 us
  transfers between devices with their start and end apart: 6, of which 3 were waited for; matrix products, arithmetic and copies ran while one was open for 17% of the time, Pallas kernels for 0%

commit v1 on v0

v1 whole, which is shorter than its diff:
```python
import functools
import math

import jax
import jax.numpy as jnp
import numpy as np
from jax import lax
from jax.experimental import pallas as pl
from jax.experimental.pallas import tpu as pltpu
from jax.sharding import PartitionSpec as P

MESH = pl.DeviceIdType.MESH
F32 = jnp.float32
BF16 = jnp.bfloat16


def dft_matrix(pulses):
    index = np.arange(pulses)
    angles = (index[:, None] * index[None, :] % pulses) * (2.0 * math.pi / pulses)
    cosine = np.cos(angles) / math.sqrt(pulses)
    sine = np.sin(angles) / math.sqrt(pulses)
    upper = np.concatenate([cosine.T, sine.T], axis=1)
    lower = np.concatenate([-sine.T, cosine.T], axis=1)
    return jnp.asarray(np.concatenate([upper, lower], axis=0), dtype=BF16)


def kernel(
    dims,
    snap_ref, spatial_ref, dft_ref, taps_ref, step_ref, trained_ref,
    err_out, taps_out,
    xbuf, spec, specb, trcol, wpad, fpad, epad, rpad, ppad,
    cur, wbuf, wrx, ebuf, erx, gf, gbuf, arx, bbuf, brx,
    x_sem, ag_send, ag_recv, er_send, er_recv, a_send, a_recv, b_send, b_recv,
):
    blocks, gates, pulses, chans, beams, dcount, rcount, chunk = dims
    nb = pulses // dcount
    lanes = 2 * gates
    nchunk = gates // chunk
    taps = 3
    slots = taps * beams
    me = lax.axis_index("doppler")
    mz = lax.axis_index("range")

    def x_copy(l, c):
        part = pl.ds(c * chunk, chunk)
        return pltpu.make_async_copy(snap_ref.at[l, part], xbuf.at[l, part], x_sem.at[l, c])

    for l in range(blocks):
        for c in range(nchunk):
            x_copy(l, c).start()

    barrier = pltpu.get_barrier_semaphore()
    for o in range(1, dcount):
        pl.semaphore_signal(barrier, inc=1, device_id={"doppler": lax.rem(me + o, dcount)}, device_id_type=MESH)
    for o in range(1, rcount):
        pl.semaphore_signal(barrier, inc=1, device_id={"range": lax.rem(mz + o, rcount)}, device_id_type=MESH)

    lane = lax.broadcasted_iota(jnp.int32, (1, lanes), 1)
    sign = jnp.where(lane < gates, 1.0, -1.0).astype(F32)
    blane = lax.broadcasted_iota(jnp.int32, (1, beams), 1)

    for j in range(taps):
        for q in range(2):
            cur[pl.ds((2 * j + q) * nb, nb), :] = taps_ref[:, q, j, :]

    def put_taps(l):
        wbuf[l, 0:6 * nb] = cur[...].astype(BF16)
        wrx[l, me, 0:6 * nb] = cur[...].astype(BF16)

    put_taps(0)
    gf[...] = jnp.zeros_like(gf)
    epad[...] = jnp.zeros_like(epad)
    rows8 = lax.broadcasted_iota(jnp.int32, (8, beams), 0)
    lane8 = lax.broadcasted_iota(jnp.int32, (8, beams), 1)
    pick = jnp.where((rows8 == 6) & (lane8 == 0), 1.0, 0.0).astype(F32)

    def init_w(m, carry):
        wpad[pl.ds(m * 8, 8), :] = pick
        return carry

    lax.fori_loop(0, pulses + 2, init_w, 0)

    pl.semaphore_wait(barrier, dcount - 1 + rcount - 1)

    def ag_copy(l, o):
        return pltpu.make_async_remote_copy(
            src_ref=wbuf.at[l], dst_ref=wrx.at[l, me],
            send_sem=ag_send.at[l, o], recv_sem=ag_recv.at[l, o],
            device_id={"doppler": lax.rem(me + o, dcount)}, device_id_type=MESH)

    def er_copy(l, o):
        peer = lax.rem(me + o, dcount)
        return pltpu.make_async_remote_copy(
            src_ref=ebuf.at[l, peer], dst_ref=erx.at[l, me],
            send_sem=er_send.at[l, o], recv_sem=er_recv.at[l, o],
            device_id={"doppler": peer}, device_id_type=MESH)

    def a_copy(l, o):
        peer = lax.rem(me + o, dcount)
        return pltpu.make_async_remote_copy(
            src_ref=gbuf.at[l, peer], dst_ref=arx.at[l, me],
            send_sem=a_send.at[l, o], recv_sem=a_recv.at[l, o],
            device_id={"doppler": peer}, device_id_type=MESH)

    def b_copy(l, o):
        return pltpu.make_async_remote_copy(
            src_ref=bbuf.at[l], dst_ref=brx.at[l, mz],
            send_sem=b_send.at[l, o], recv_sem=b_recv.at[l, o],
            device_id={"range": lax.rem(mz + o, rcount)}, device_id_type=MESH)

    def spectra(l, first, last):
        def step(c, carry):
            x_copy(l, c).wait()
            x = xbuf[l, pl.ds(c * chunk, chunk)]
            lhs = jnp.concatenate(
                [x[:, 0].reshape(chunk * pulses, chans), x[:, 1].reshape(chunk * pulses, chans)], axis=1)
            y = jnp.dot(lhs, spatial_ref[...], preferred_element_type=F32).astype(BF16)
            cols = []
            for g in range(chunk):
                one = y[g * pulses:(g + 1) * pulses]
                cols.append(jnp.concatenate([one[:, :beams], one[:, beams:]], axis=0))
            o = jnp.dot(dft_ref[...], jnp.concatenate(cols, axis=1), preferred_element_type=F32)
            for g in range(chunk):
                for t in range(2):
                    spec[pl.ds(t * gates + c * chunk + g, pulses, stride=lanes), :] = (
                        o[t * pulses:(t + 1) * pulses, g * beams:(g + 1) * beams])
            return carry

        lax.fori_loop(first, last, step, 0)

    def pack(l):
        row = trained_ref[pl.ds(l, 1), :]
        trcol[...] = jnp.transpose(jnp.broadcast_to(row, (lanes, lanes)))[:, :1] * jnp.ones((1, beams), F32)

        def step(m, carry):
            s = spec[pl.ds(m * lanes, lanes), :].astype(BF16)
            specb[m] = s
            wide = s.astype(F32)
            sq = wide * wide * trcol[...]
            ppad[pl.ds((m + 1) * 8, 8), :] = jnp.sum(sq.reshape(lanes // 8, 8, beams), axis=0)
            return carry

        lax.fori_loop(0, pulses, step, 0, unroll=4)
        ppad[0:8] = ppad[pulses * 8:pulses * 8 + 8]
        ppad[(pulses + 1) * 8:(pulses + 2) * 8] = ppad[8:16]

    def build_w(l):
        for d in range(dcount):
            part = wrx[l, d].astype(F32)
            for j in range(taps):
                for q in range(2):
                    r = 2 * j + q
                    val = part[r * nb:(r + 1) * nb]
                    if j == 1:
                        val = jnp.where(blane == 0, 0.0, val)
                    wpad[pl.ds((d * nb + j) * 8 + r, nb, stride=8), :] = val
        wrap(wpad)

    def wrap(ref):
        ref[pulses * 8:pulses * 8 + 2] = ref[0:2]
        ref[12:14] = ref[(pulses + 1) * 8 + 4:(pulses + 1) * 8 + 6]

    def errors(l):
        def step(m, carry):
            w = wpad[pl.ds((m + 1) * 8, 8), :].astype(BF16)
            fpad[pl.ds((m + 1) * 8, 8), :] = lax.dot_general(
                w, specb[m], (((1,), (1,)), ((), ())), preferred_element_type=F32)
            return carry

        lax.fori_loop(0, pulses, step, 0, unroll=8)
        fpad[0:8] = fpad[pulses * 8:pulses * 8 + 8]
        fpad[(pulses + 1) * 8:(pulses + 2) * 8] = fpad[8:16]
        total = jnp.zeros((pulses, lanes), F32)
        for j in range(taps):
            f0 = fpad[pl.ds(j * 8 + 2 * j, pulses, stride=8), :]
            f1 = fpad[pl.ds(j * 8 + 2 * j + 1, pulses, stride=8), :]
            total = total + f0 + sign * pltpu.roll(f1, gates, 1)
        main = fpad[pl.ds(8 + 6, pulses, stride=8), :]
        err = main - (1.0 / math.sqrt(slots)) * total
        for d in range(dcount):
            ebuf[l, d] = err[d * nb:(d + 1) * nb]
        erx[l, me] = ebuf[l, me]
        for o in range(1, dcount):
            er_copy(l, o).start()
        e0 = err.astype(BF16).astype(F32) * trained_ref[pl.ds(l, 1), :]
        e1 = -sign * pltpu.roll(e0, gates, 1)
        for j in range(taps):
            epad[pl.ds(j * 8 + 2 * j, pulses, stride=8), :] = e0
            epad[pl.ds(j * 8 + 2 * j + 1, pulses, stride=8), :] = e1
        wrap(epad)

    def gradient(l):
        def step(m, carry):
            e = epad[pl.ds((m + 1) * 8, 8), :].astype(BF16)
            rpad[pl.ds((m + 1) * 8, 8), :] = jnp.dot(e, specb[m], preferred_element_type=F32)
            return carry

        lax.fori_loop(0, pulses, step, 0, unroll=8)
        rpad[0:8] = rpad[pulses * 8:pulses * 8 + 8]
        rpad[(pulses + 1) * 8:(pulses + 2) * 8] = rpad[8:16]
        for j in range(taps):
            for q in range(2):
                r = 2 * j + q
                val = rpad[pl.ds(j * 8 + r, pulses, stride=8), :]
                if j == 1:
                    val = jnp.where(blane == 0, 0.0, val)
                for d in range(dcount):
                    gf[d, r * nb:(r + 1) * nb] = val[d * nb:(d + 1) * nb]
        power = jnp.zeros((pulses, beams), F32)
        for j in range(taps):
            one = jnp.zeros((pulses, beams), F32)
            for i in range(8):
                one = one + ppad[pl.ds(j * 8 + i, pulses, stride=8), :]
            if j == 1:
                one = jnp.where(blane == 0, 0.0, one)
            power = power + one
        for d in range(dcount):
            gf[d, 6 * nb:7 * nb] = power[d * nb:(d + 1) * nb]
        gbuf[l] = gf[...].astype(BF16)
        for o in range(1, dcount):
            a_copy(l, o).start()

    def reduce_a(l):
        total = gf[me]
        for o in range(1, dcount):
            a_copy(l, o).wait_recv()
            total = total + arx[l, lax.rem(me + dcount - o, dcount)].astype(F32)
        narrow = total.astype(BF16)
        bbuf[l] = narrow
        brx[l, mz] = narrow
        for o in range(1, rcount):
            b_copy(l, o).start()

    def reduce_b(l):
        for o in range(1, rcount):
            b_copy(l, o).wait_recv()
        total = brx[l, 0].astype(F32)
        for z in range(1, rcount):
            total = total + brx[l, z].astype(F32)
        power = jnp.sum(total[6 * nb:7 * nb], axis=1, keepdims=True)
        rows = lax.broadcasted_iota(jnp.int32, (nb, 1), 0)
        steps = jnp.zeros((nb, 1), F32)
        for i in range(nb):
            steps = jnp.where(rows == i, step_ref[i], steps)
        factor = steps * math.sqrt(slots) / (power / slots + 1e-06)
        for r in range(6):
            part = pl.ds(r * nb, nb)
            cur[part, :] = cur[part, :] + factor * total[r * nb:(r + 1) * nb]

    def send_taps(l):
        for o in range(1, dcount):
            ag_copy(l, o).start()

    def await_taps(l):
        for o in range(1, dcount):
            ag_copy(l, o).wait_recv()
        build_w(l)

    send_taps(0)
    spectra(0, 0, nchunk)
    pack(0)
    await_taps(0)
    for l in range(blocks):
        errors(l)
        gradient(l)
        if l + 1 < blocks:
            spectra(l + 1, 0, nchunk // 2)
            reduce_a(l)
            spectra(l + 1, nchunk // 2, nchunk)
            reduce_b(l)
            put_taps(l + 1)
            send_taps(l + 1)
            pack(l + 1)
            await_taps(l + 1)
        else:
            for k in range(blocks):
                for o in range(1, dcount):
                    er_copy(k, o).wait_recv()
                for i in range(dcount // 2):
                    low = erx[k, 2 * i]
                    high = erx[k, 2 * i + 1]
                    part = pl.ds(i * lanes, lanes)
                    err_out[k, 0, :, part] = jnp.where(lane < gates, low, pltpu.roll(high, gates, 1))
                    err_out[k, 1, :, part] = jnp.where(lane < gates, pltpu.roll(low, gates, 1), high)
            reduce_a(l)
            reduce_b(l)
    for j in range(taps):
        for q in range(2):
            taps_out[:, q, j, :] = cur[pl.ds((2 * j + q) * nb, nb), :]
    for l in range(blocks):
        for o in range(1, dcount):
            ag_copy(l, o).wait_send()
            er_copy(l, o).wait_send()
            a_copy(l, o).wait_send()
        for o in range(1, rcount):
            b_copy(l, o).wait_send()


def body(snapshot, spatial, tap_weights, step_size, train_mask, guard_center):
    blocks, gates, _, pulses, chans = snapshot.shape
    beams = spatial.shape[3]
    rcount = lax.axis_size("range")
    dcount = lax.axis_size("doppler")
    nb = pulses // dcount
    lanes = 2 * gates
    chunk = math.gcd(gates, 8)
    nchunk = gates // chunk
    guard_width = gates * rcount * dcount // 8
    start = lax.axis_index("doppler") * gates
    mine = lax.dynamic_slice_in_dim(train_mask, start, gates, axis=1)
    positions = lax.axis_index("range") * (gates * dcount) + start + jnp.arange(gates, dtype=jnp.int32)
    outside = jnp.abs(positions[None, :] - guard_center[:, None]) > guard_width
    trained = jnp.where(outside, mine, 0).astype(F32)
    trained = jnp.concatenate([trained, trained], axis=1)
    wrows = -(-6 * nb // 16) * 16
    dims = (blocks, gates, pulses, chans, beams, dcount, rcount, chunk)
    vmem = pl.BlockSpec(memory_space=pltpu.VMEM)
    dma = pltpu.SemaphoreType.DMA
    pad = (pulses + 2) * 8
    return pl.pallas_call(
        functools.partial(kernel, dims),
        out_shape=(
            jax.ShapeDtypeStruct((blocks, 2, nb, gates * dcount), F32),
            jax.ShapeDtypeStruct((nb, 2, 3, beams), F32),
        ),
        in_specs=[
            pl.BlockSpec(memory_space=pl.ANY), vmem, vmem, vmem,
            pl.BlockSpec(memory_space=pltpu.SMEM), vmem,
        ],
        out_specs=(vmem, vmem),
        scratch_shapes=[
            pltpu.VMEM((blocks, gates, 2, pulses, chans), BF16),
            pltpu.VMEM((pulses * lanes, beams), F32),
            pltpu.VMEM((pulses, lanes, beams), BF16),
            pltpu.VMEM((lanes, beams), F32),
            pltpu.VMEM((pad, beams), F32),
            pltpu.VMEM((pad, lanes), F32),
            pltpu.VMEM((pad, lanes), F32),
            pltpu.VMEM((pad, beams), F32),
            pltpu.VMEM((pad, beams), F32),
            pltpu.VMEM((6 * nb, beams), F32),
            pltpu.VMEM((blocks, wrows, beams), BF16),
            pltpu.VMEM((blocks, dcount, wrows, beams), BF16),
            pltpu.VMEM((blocks, dcount, nb, lanes), F32),
            pltpu.VMEM((blocks, dcount, nb, lanes), F32),
            pltpu.VMEM((dcount, 8 * nb, beams), F32),
            pltpu.VMEM((blocks, dcount, 8 * nb, beams), BF16),
            pltpu.VMEM((blocks, dcount, 8 * nb, beams), BF16),
            pltpu.VMEM((blocks, 8 * nb, beams), BF16),
            pltpu.VMEM((blocks, rcount, 8 * nb, beams), BF16),
            dma((blocks, nchunk)),
            dma((blocks, dcount)), dma((blocks, dcount)),
            dma((blocks, dcount)), dma((blocks, dcount)),
            dma((blocks, dcount)), dma((blocks, dcount)),
            dma((blocks, rcount)), dma((blocks, rcount)),
        ],
        compiler_params=pltpu.CompilerParams(collective_id=0, has_side_effects=True),
    )(
        snapshot,
        spatial.reshape(2 * chans, 2 * beams),
        dft_matrix(pulses),
        tap_weights,
        step_size,
        trained,
    )


def solution(mesh):
    return jax.shard_map(
        body,
        mesh=mesh,
        in_specs=(
            P(None, ("range", "doppler"), None, None, None),
            P(),
            P("doppler", None, None, None),
            P("doppler"),
            P(None, "range"),
            P(),
        ),
        out_specs=(P(None, None, "doppler", "range"), P("doppler", None, None, None)),
        check_vma=False,
    )
```

time: 155 us -> 48.9 us (0.32)
  waiting for transfers between devices: 41.5 us -> 0 us
  Pallas kernels: 0 us -> 40.7 us
  blocking collectives: 35.1 us -> 0 us
  matrix products: 24.1 us -> 0 us
  local copies, waits for them, and re-layouts: 23.8 us -> 5.78 us
  starting transfers between devices: 14.8 us -> 0 us
  other arithmetic: 14 us -> 1.4 us
    pallas_call x0 -> x1, Pallas kernels: none -> 40.7 us  [body(): pl.pallas_call(functools.partial(kernel, dims), out_shape=(jax.ShapeDtype...]
    all_to_all x2 -> x0, waiting for transfers between devices: 35.8 us -> none  [body(): lax.all_to_all(spectra, 'doppler', split_axis=2, concat_axis=0, tiled=True)]
    psum x2 -> x0, blocking collectives: 35.1 us -> none  [body(): gradient, power_sum = lax.psum((gradient, power_sum), 'range')]
    dot_general x8 -> x0, matrix products: 24.1 us -> none  [the longest x2 9.12 us: canceller(): jnp.einsum('rskjb,kqjb->rskq', auxiliary, weights, preferred_element_type...]
    all_to_all x2 -> x0, starting transfers between devices: 9.54 us -> none  [body(): lax.all_to_all(spectra, 'doppler', split_axis=2, concat_axis=0, tiled=True)]
    convert_element_type x2 -> x0, local copies, waits for them, and re-layouts: 6.97 us -> none  [to_bins(): return jnp.einsum('gspb,sptk->gtkb', beam_data, transform, preferred_elem...]
    dot_general x1 -> x0, other arithmetic: 6 us -> none  [canceller(): jnp.einsum('rskjb,rskjb->rk', auxiliary, auxiliary, preferred_element_typ...]
    all_to_all x2 -> x0, local copies, waits for them, and re-layouts: 5.91 us -> none  [body(): lax.all_to_all(spectra, 'doppler', split_axis=2, concat_axis=0, tiled=True)]
  transfers between devices with their start and end apart: 6 -> 0, of which waited for: 3 -> 0; matrix products, arithmetic and copies ran while one was open for 17% -> 0% of each run, Pallas kernels for 0% -> 0%
where the time goes in v1:
time: 48.9 us; the launch traced here: 48.6 us
  Pallas kernels  40.7 us (83%)
  local copies, waits for them, and re-layouts  5.78 us (12%)
  other arithmetic  1.4 us (3%)
  between operations  0.65 us (1%)
    pallas_call x1, Pallas kernels, body(): pl.pallas_call(functools.partial(kernel, dims), out_shape=(jax.ShapeDtype...  40.7 us
    unnamed x3, local copies, waits for them, and re-layouts  4.4 us
    pallas_call x1, local copies, waits for them, and re-layouts, body(): pl.pallas_call(functools.partial(kernel, dims), out_shape=(jax.ShapeDtype...  1.38 us

profile of v1, /device:TPU:0, one launch (start us, length us, event | category | flops | bytes accessed | tf_op | source)
XLA Modules:
  0.0 48.6 jit_solution(10985784751452764385)
XLA Ops:
  0.6 0.8 %fusion = f32[2,64]{1,0:T(2,128)S(1)} fusion(s32[2,512]{1,0:T(2,128)} %param.11, s32[]{:T(128)S(6)} %select_n.7, s32[64]{0:T(128)S(1)} %iota_add_fusion, s32[2]{0:T(128)} %param.12), kind=kLoop, calls=%fused_computation.2 | loop fusion | flops 640 | bytes 1292 | tf_op jit(solution)/shard_map/convert_element_type | solution.py:313
  1.4 0.6 %pad_maximum_fusion.trained_ref = f32[2,128]{1,0:T(2,128)} fusion(f32[2,64]{1,0:T(2,128)S(1)} %fusion), kind=kLoop, calls=%fused_computation.3 | loop fusion | flops 256 | bytes 1536 | tf_op jit(solution)/shard_map/concatenate | solution.py:314
  2.0 1.4 %copy.9.taps_ref = f32[8,2,3,128]{3,2,1,0:T(4,128)} copy(f32[8,2,3,128]{3,1,2,0:T(2,128)} %param.9) | data formatting | bytes 49152 | tf_op args[2]
  3.4 1.6 %copy.13 = bf16[32,8,2,128]{3,1,2,0:T(8,128)(2,1)} copy(bf16[32,8,2,128]{3,2,1,0:T(2,128)(2,1)} %bitcast.6) | data formatting | bytes 262144
  5.0 40.7 %shard_map.86 = (f32[2,2,8,512]{3,2,1,0:T(8,128)}, f32[8,2,3,128]{3,2,1,0:T(4,128)}) custom-call(bf16[2,64,2,64,128]{4,3,2,1,0:T(8,128)(2,1)} %snap_ref.1, bf16[256,256]{1,0:T(8,128)(2,1)} %bitcast.5, bf16[128,128]{1,0:T(8,128)(2,1)} %constant.18.clone.dft_ref, f32[8,2,3,128]{3,2,1,0:T(4,128)} %copy.9.taps_ref, f32[8]{0:T(128)} %step_ref.1, ...), custom_call_target="tpu_custom_call" | custom-call | tf_op jit(solution)/shard_map/pallas_call | solution.py:320
  45.7 1.4 %copy.10 = f32[8,2,3,128]{3,1,2,0:T(2,128)} copy(f32[8,2,3,128]{3,2,1,0:T(4,128)} %get-tuple-element.3) | data formatting | bytes 49152 | tf_op jit(solution)/shard_map/pallas_call | solution.py:320
  47.1 1.5 %copy.15 = f32[2,2,8,512]{3,2,1,0:T(8,128)} copy(f32[2,2,8,512]{3,2,1,0:T(8,128)} %get-tuple-element.6) | data formatting | bytes 131072
  (1 shorter events, 0.0 us)

commit v2 on v1

--- a/solution.py
+++ b/solution.py
@@ -26,15 +26,16 @@
 
 def kernel(
     dims,
-    snap_ref, spatial_ref, dft_ref, taps_ref, step_ref, trained_ref,
+    snap_ref, spatial_ref, dft_ref, taps_ref, step_ref, mask_ref, guard_ref,
     err_out, taps_out,
-    xbuf, spec, specb, trcol, wpad, fpad, epad, rpad, ppad,
+    xbuf, spec, trained, wpad, fpad, epad, rpad, smat,
     cur, wbuf, wrx, ebuf, erx, gf, gbuf, arx, bbuf, brx,
     x_sem, ag_send, ag_recv, er_send, er_recv, a_send, a_recv, b_send, b_recv,
 ):
     blocks, gates, pulses, chans, beams, dcount, rcount, chunk = dims
     nb = pulses // dcount
     lanes = 2 * gates
+    pitch = lanes + 8
     nchunk = gates // chunk
     taps = 3
     slots = taps * beams
@@ -61,7 +62,24 @@
 
     for j in range(taps):
         for q in range(2):
-            cur[pl.ds((2 * j + q) * nb, nb), :] = taps_ref[:, q, j, :]
+            cur[pl.ds((2 * j + q) * nb, nb), :] = taps_ref[:, j, q, :]
+
+    mask = jnp.zeros((blocks, lanes), jnp.int32)
+    for i in range(dcount // 2):
+        mask = jnp.where(me // 2 == i, mask_ref[:, i * lanes:(i + 1) * lanes], mask)
+    swapped = pltpu.roll(mask, gates, 1)
+    even = jnp.where(lane < gates, mask, swapped)
+    odd = jnp.where(lane < gates, swapped, mask)
+    mask = jnp.where(lax.rem(me, 2) == 0, even, odd)
+    position = (mz * dcount + me) * gates + jnp.where(lane < gates, lane, lane - gates)
+    guard_width = gates * rcount * dcount // 8
+    for l in range(blocks):
+        outside = jnp.abs(position - guard_ref[l]) > guard_width
+        trained[l:l + 1, :] = jnp.where(outside, mask[l:l + 1], 0).astype(F32)
+
+    for r in range(2):
+        for s in range(2):
+            smat[r * chans:(r + 1) * chans, s * beams:(s + 1) * beams] = spatial_ref[r, :, s, :]
 
     def put_taps(l):
         wbuf[l, 0:6 * nb] = cur[...].astype(BF16)
@@ -114,7 +132,7 @@
             x = xbuf[l, pl.ds(c * chunk, chunk)]
             lhs = jnp.concatenate(
                 [x[:, 0].reshape(chunk * pulses, chans), x[:, 1].reshape(chunk * pulses, chans)], axis=1)
-            y = jnp.dot(lhs, spatial_ref[...], preferred_element_type=F32).astype(BF16)
+            y = jnp.dot(lhs, smat[...], preferred_element_type=F32).astype(BF16)
             cols = []
             for g in range(chunk):
                 one = y[g * pulses:(g + 1) * pulses]
@@ -122,27 +140,14 @@
             o = jnp.dot(dft_ref[...], jnp.concatenate(cols, axis=1), preferred_element_type=F32)
             for g in range(chunk):
                 for t in range(2):
-                    spec[pl.ds(t * gates + c * chunk + g, pulses, stride=lanes), :] = (
+                    spec[pl.ds(t * gates + c * chunk + g, pulses, stride=pitch), :] = (
                         o[t * pulses:(t + 1) * pulses, g * beams:(g + 1) * beams])
             return carry
 
         lax.fori_loop(first, last, step, 0)
 
-    def pack(l):
-        row = trained_ref[pl.ds(l, 1), :]
-        trcol[...] = jnp.transpose(jnp.broadcast_to(row, (lanes, lanes)))[:, :1] * jnp.ones((1, beams), F32)
-
-        def step(m, carry):
-            s = spec[pl.ds(m * lanes, lanes), :].astype(BF16)
-            specb[m] = s
-            wide = s.astype(F32)
-            sq = wide * wide * trcol[...]
-            ppad[pl.ds((m + 1) * 8, 8), :] = jnp.sum(sq.reshape(lanes // 8, 8, beams), axis=0)
-            return carry
-
-        lax.fori_loop(0, pulses, step, 0, unroll=4)
-        ppad[0:8] = ppad[pulses * 8:pulses * 8 + 8]
-        ppad[(pulses + 1) * 8:(pulses + 2) * 8] = ppad[8:16]
+    def bin_spectra(m):
+        return spec[pl.ds(pl.multiple_of(m * pitch, 8), lanes), :].astype(BF16)
 
     def build_w(l):
         for d in range(dcount):
@@ -161,13 +166,16 @@
         ref[12:14] = ref[(pulses + 1) * 8 + 4:(pulses + 1) * 8 + 6]
 
     def errors(l):
-        def step(m, carry):
-            w = wpad[pl.ds((m + 1) * 8, 8), :].astype(BF16)
-            fpad[pl.ds((m + 1) * 8, 8), :] = lax.dot_general(
-                w, specb[m], (((1,), (1,)), ((), ())), preferred_element_type=F32)
+        def step(i, carry):
+            m = 2 * i
+            w = wpad[pl.ds(pl.multiple_of((m + 1) * 8, 8), 16), :].astype(BF16)
+            pair = jnp.concatenate([bin_spectra(m), bin_spectra(m + 1)], axis=0)
+            f = lax.dot_general(w, pair, (((1,), (1,)), ((), ())), preferred_element_type=F32)
+            fpad[pl.ds(pl.multiple_of((m + 1) * 8, 8), 8), :] = f[:8, :lanes]
+            fpad[pl.ds(pl.multiple_of((m + 2) * 8, 8), 8), :] = f[8:, lanes:]
             return carry
 
-        lax.fori_loop(0, pulses, step, 0, unroll=8)
+        lax.fori_loop(0, pulses // 2, step, 0, unroll=8)
         fpad[0:8] = fpad[pulses * 8:pulses * 8 + 8]
         fpad[(pulses + 1) * 8:(pulses + 2) * 8] = fpad[8:16]
         total = jnp.zeros((pulses, lanes), F32)
@@ -182,7 +190,7 @@
         erx[l, me] = ebuf[l, me]
         for o in range(1, dcount):
             er_copy(l, o).start()
-        e0 = err.astype(BF16).astype(F32) * trained_ref[pl.ds(l, 1), :]
+        e0 = err.astype(BF16).astype(F32) * trained[l:l + 1, :]
         e1 = -sign * pltpu.roll(e0, gates, 1)
         for j in range(taps):
             epad[pl.ds(j * 8 + 2 * j, pulses, stride=8), :] = e0
@@ -190,9 +198,15 @@
         wrap(epad)
 
     def gradient(l):
+        rows = lax.broadcasted_iota(jnp.int32, (8, lanes), 0)
+        keep = jnp.where(rows == 6, trained[l:l + 1, :], 0.0).astype(BF16)
+
         def step(m, carry):
-            e = epad[pl.ds((m + 1) * 8, 8), :].astype(BF16)
-            rpad[pl.ds((m + 1) * 8, 8), :] = jnp.dot(e, specb[m], preferred_element_type=F32)
+            part = pl.ds(pl.multiple_of((m + 1) * 8, 8), 8)
+            e = jnp.concatenate([epad[part, :].astype(BF16), keep], axis=1)
+            one = bin_spectra(m)
+            both = jnp.concatenate([one, one * one], axis=0)
+            rpad[part, :] = jnp.dot(e, both, preferred_element_type=F32)
             return carry
 
         lax.fori_loop(0, pulses, step, 0, unroll=8)
@@ -208,9 +222,7 @@
                     gf[d, r * nb:(r + 1) * nb] = val[d * nb:(d + 1) * nb]
         power = jnp.zeros((pulses, beams), F32)
         for j in range(taps):
-            one = jnp.zeros((pulses, beams), F32)
-            for i in range(8):
-                one = one + ppad[pl.ds(j * 8 + i, pulses, stride=8), :]
+            one = rpad[pl.ds(j * 8 + 6, pulses, stride=8), :]
             if j == 1:
                 one = jnp.where(blane == 0, 0.0, one)
             power = power + one
@@ -258,7 +270,6 @@
 
     send_taps(0)
     spectra(0, 0, nchunk)
-    pack(0)
     await_taps(0)
     for l in range(blocks):
         errors(l)
@@ -270,7 +281,6 @@
             reduce_b(l)
             put_taps(l + 1)
             send_taps(l + 1)
-            pack(l + 1)
             await_taps(l + 1)
         else:
             for k in range(blocks):
@@ -286,7 +296,7 @@
             reduce_b(l)
     for j in range(taps):
         for q in range(2):
-            taps_out[:, q, j, :] = cur[pl.ds((2 * j + q) * nb, nb), :]
+            taps_out[:, j, q, :] = cur[pl.ds((2 * j + q) * nb, nb), :]
     for l in range(blocks):
         for o in range(1, dcount):
             ag_copy(l, o).wait_send()
@@ -305,39 +315,31 @@
     lanes = 2 * gates
     chunk = math.gcd(gates, 8)
     nchunk = gates // chunk
-    guard_width = gates * rcount * dcount // 8
-    start = lax.axis_index("doppler") * gates
-    mine = lax.dynamic_slice_in_dim(train_mask, start, gates, axis=1)
-    positions = lax.axis_index("range") * (gates * dcount) + start + jnp.arange(gates, dtype=jnp.int32)
-    outside = jnp.abs(positions[None, :] - guard_center[:, None]) > guard_width
-    trained = jnp.where(outside, mine, 0).astype(F32)
-    trained = jnp.concatenate([trained, trained], axis=1)
     wrows = -(-6 * nb // 16) * 16
     dims = (blocks, gates, pulses, chans, beams, dcount, rcount, chunk)
     vmem = pl.BlockSpec(memory_space=pltpu.VMEM)
     dma = pltpu.SemaphoreType.DMA
     pad = (pulses + 2) * 8
-    return pl.pallas_call(
+    errors, taps = pl.pallas_call(
         functools.partial(kernel, dims),
         out_shape=(
             jax.ShapeDtypeStruct((blocks, 2, nb, gates * dcount), F32),
-            jax.ShapeDtypeStruct((nb, 2, 3, beams), F32),
+            jax.ShapeDtypeStruct((nb, 3, 2, beams), F32),
         ),
         in_specs=[
             pl.BlockSpec(memory_space=pl.ANY), vmem, vmem, vmem,
-            pl.BlockSpec(memory_space=pltpu.SMEM), vmem,
+            pl.BlockSpec(memory_space=pltpu.SMEM), vmem, pl.BlockSpec(memory_space=pltpu.SMEM),
         ],
         out_specs=(vmem, vmem),
         scratch_shapes=[
             pltpu.VMEM((blocks, gates, 2, pulses, chans), BF16),
-            pltpu.VMEM((pulses * lanes, beams), F32),
-            pltpu.VMEM((pulses, lanes, beams), BF16),
-            pltpu.VMEM((lanes, beams), F32),
+            pltpu.VMEM((pulses * (lanes + 8), beams), F32),
+            pltpu.VMEM((blocks, lanes), F32),
             pltpu.VMEM((pad, beams), F32),
             pltpu.VMEM((pad, lanes), F32),
             pltpu.VMEM((pad, lanes), F32),
             pltpu.VMEM((pad, beams), F32),
-            pltpu.VMEM((pad, beams), F32),
+            pltpu.VMEM((2 * chans, 2 * beams), BF16),
             pltpu.VMEM((6 * nb, beams), F32),
             pltpu.VMEM((blocks, wrows, beams), BF16),
             pltpu.VMEM((blocks, dcount, wrows, beams), BF16),
@@ -357,12 +359,14 @@
         compiler_params=pltpu.CompilerParams(collective_id=0, has_side_effects=True),
     )(
         snapshot,
-        spatial.reshape(2 * chans, 2 * beams),
+        spatial,
         dft_matrix(pulses),
-        tap_weights,
+        jnp.transpose(tap_weights, (0, 2, 1, 3)),
         step_size,
-        trained,
+        train_mask,
+        guard_center,
     )
+    return (errors, jnp.transpose(taps, (0, 2, 1, 3)))
 
 
 def solution(mesh):

time: 48.9 us -> 39.6 us (0.81)
  Pallas kernels: 40.7 us -> 35.9 us
  local copies, waits for them, and re-layouts: 5.78 us -> 2.82 us
  other arithmetic: 1.4 us -> 0 us
    pallas_call x1, Pallas kernels: 40.7 us -> 35.9 us  [body(): pl.pallas_call(functools.partial(kernel, dims), out_shape=(jax.ShapeDtype...]
    unnamed x3 -> x2, local copies, waits for them, and re-layouts: 4.4 us -> 2.82 us
    pallas_call x1 -> x0, local copies, waits for them, and re-layouts: 1.38 us -> none  [body(): pl.pallas_call(functools.partial(kernel, dims), out_shape=(jax.ShapeDtype...]
    convert_element_type x1 -> x0, other arithmetic: 0.76 us -> none  [body(): trained = jnp.where(outside, mine, 0).astype(F32)]
    concatenate x1 -> x0, other arithmetic: 0.64 us -> none  [body(): trained = jnp.concatenate([trained, trained], axis=1)]
where the time goes in v2:
time: 39.6 us; the launch traced here: 39.4 us
  Pallas kernels  35.9 us (91%)
  local copies, waits for them, and re-layouts  2.82 us (7%)
  between operations  0.64 us (2%)
    pallas_call x1, Pallas kernels, body(): pl.pallas_call(functools.partial(kernel, dims), out_shape=(jax.ShapeDtype...  35.9 us
    unnamed x2, local copies, waits for them, and re-layouts  2.82 us

profile of v2, /device:TPU:0, one launch (start us, length us, event | category | flops | bytes accessed | tf_op | source)
XLA Modules:
  0.0 39.4 jit_solution(18381327227073996481)
XLA Ops:
  0.6 35.9 %shard_map.86 = (f32[2,2,8,512]{3,2,1,0:T(8,128)}, f32[8,3,2,128]{3,2,1,0:T(2,128)}) custom-call(bf16[2,64,2,64,128]{4,3,2,1,0:T(8,128)(2,1)} %snap_ref.1, bf16[2,128,2,128]{3,2,1,0:T(2,128)(2,1)} %spatial_ref.1, bf16[128,128]{1,0:T(8,128)(2,1)} %constant.2.clone.dft_ref, f32[8,3,2,128]{3,2,1,0:T(2,128)} %bitcast.2, f32[8]{0:T(128)} %step_ref.1, ...), custom_call_target="tpu_custom_call" | custom-call | tf_op jit(solution)/shard_map/pallas_call | solution.py:323
  36.6 1.5 %copy.11 = f32[2,2,8,512]{3,2,1,0:T(8,128)} copy(f32[2,2,8,512]{3,2,1,0:T(8,128)} %get-tuple-element.8) | data formatting | bytes 131072
  38.0 1.4 %copy.12 = f32[8,2,3,128]{3,1,2,0:T(2,128)} copy(f32[8,2,3,128]{3,1,2,0:T(2,128)} %bitcast.3) | data formatting | bytes 49152

commit v3 on v2

--- a/solution.py
+++ b/solution.py
@@ -98,8 +98,6 @@
 
     lax.fori_loop(0, pulses + 2, init_w, 0)
 
-    pl.semaphore_wait(barrier, dcount - 1 + rcount - 1)
-
     def ag_copy(l, o):
         return pltpu.make_async_remote_copy(
             src_ref=wbuf.at[l], dst_ref=wrx.at[l, me],
@@ -175,7 +173,7 @@
             fpad[pl.ds(pl.multiple_of((m + 2) * 8, 8), 8), :] = f[8:, lanes:]
             return carry
 
-        lax.fori_loop(0, pulses // 2, step, 0, unroll=8)
+        lax.fori_loop(0, pulses // 2, step, 0, unroll=16)
         fpad[0:8] = fpad[pulses * 8:pulses * 8 + 8]
         fpad[(pulses + 1) * 8:(pulses + 2) * 8] = fpad[8:16]
         total = jnp.zeros((pulses, lanes), F32)
@@ -209,7 +207,7 @@
             rpad[part, :] = jnp.dot(e, both, preferred_element_type=F32)
             return carry
 
-        lax.fori_loop(0, pulses, step, 0, unroll=8)
+        lax.fori_loop(0, pulses, step, 0, unroll=16)
         rpad[0:8] = rpad[pulses * 8:pulses * 8 + 8]
         rpad[(pulses + 1) * 8:(pulses + 2) * 8] = rpad[8:16]
         for j in range(taps):
@@ -268,8 +266,11 @@
             ag_copy(l, o).wait_recv()
         build_w(l)
 
+    early = nchunk // 4
+    spectra(0, 0, early)
+    pl.semaphore_wait(barrier, dcount - 1 + rcount - 1)
     send_taps(0)
-    spectra(0, 0, nchunk)
+    spectra(0, early, nchunk)
     await_taps(0)
     for l in range(blocks):
         errors(l)
@@ -306,6 +307,11 @@
             b_copy(l, o).wait_send()
 
 
+def finish(err_ref, taps_ref, err_out, taps_out):
+    err_out[...] = err_ref[...]
+    taps_out[...] = taps_ref[...]
+
+
 def body(snapshot, spatial, tap_weights, step_size, train_mask, guard_center):
     blocks, gates, _, pulses, chans = snapshot.shape
     beams = spatial.shape[3]
@@ -313,7 +319,7 @@
     dcount = lax.axis_size("doppler")
     nb = pulses // dcount
     lanes = 2 * gates
-    chunk = math.gcd(gates, 8)
+    chunk = math.gcd(gates, 16)
     nchunk = gates // chunk
     wrows = -(-6 * nb // 16) * 16
     dims = (blocks, gates, pulses, chans, beams, dcount, rcount, chunk)
@@ -366,6 +372,15 @@
         train_mask,
         guard_center,
     )
+    errors, taps = pl.pallas_call(
+        finish,
+        out_shape=(
+            jax.ShapeDtypeStruct(errors.shape, F32),
+            jax.ShapeDtypeStruct(taps.shape, F32),
+        ),
+        in_specs=[vmem, vmem],
+        out_specs=(vmem, vmem),
+    )(errors, taps)
     return (errors, jnp.transpose(taps, (0, 2, 1, 3)))
 
 

time: 39.6 us -> 36.1 us (0.912)
  local copies, waits for them, and re-layouts: 2.82 us -> 0 us
  Pallas kernels: 35.9 us -> 35.3 us
    unnamed x2 -> x0, local copies, waits for them, and re-layouts: 2.82 us -> none
    pallas_call x1, Pallas kernels: 35.9 us -> 33.8 us  [body(): pl.pallas_call(functools.partial(kernel, dims), out_shape=(jax.ShapeDtype...]
    pallas_call x0 -> x1, Pallas kernels: none -> 1.48 us  [body(): pl.pallas_call(finish, out_shape=(jax.ShapeDtypeStruct(errors.shape, F32)...]
where the time goes in v3:
time: 36.1 us; the launch traced here: 35.9 us
  Pallas kernels  35.3 us (98%)
  between operations  0.64 us (2%)
    pallas_call x1, Pallas kernels, body(): pl.pallas_call(functools.partial(kernel, dims), out_shape=(jax.ShapeDtype...  33.8 us
    pallas_call x1, Pallas kernels, body(): pl.pallas_call(finish, out_shape=(jax.ShapeDtypeStruct(errors.shape, F32)...  1.48 us

profile of v3, /device:TPU:0, one launch (start us, length us, event | category | flops | bytes accessed | tf_op | source)
XLA Modules:
  0.0 35.9 jit_solution(18385751419932059402)
XLA Ops:
  0.6 33.8 %shard_map.86 = (f32[2,2,8,512]{3,2,1,0:T(8,128)}, f32[8,3,2,128]{3,2,1,0:T(2,128)}) custom-call(bf16[2,64,2,64,128]{4,3,2,1,0:T(8,128)(2,1)} %snap_ref.1, bf16[2,128,2,128]{3,2,1,0:T(2,128)(2,1)} %spatial_ref.1, bf16[128,128]{1,0:T(8,128)(2,1)} %constant.2.clone.dft_ref, f32[8,3,2,128]{3,2,1,0:T(2,128)} %bitcast.2, f32[8]{0:T(128)} %step_ref.1, ...), custom_call_target="tpu_custom_call" | custom-call | tf_op jit(solution)/shard_map/pallas_call | solution.py:329
  34.4 1.5 %shard_map.87 = (f32[2,2,8,512]{3,2,1,0:T(8,128)}, f32[8,3,2,128]{3,2,1,0:T(2,128)}) custom-call(f32[2,2,8,512]{3,2,1,0:T(8,128)} %get-tuple-element.6.err_ref, f32[8,3,2,128]{3,2,1,0:T(2,128)} %get-tuple-element.7.taps_ref), custom_call_target="tpu_custom_call" | custom-call | tf_op jit(solution)/shard_map/pallas_call | solution.py:375
